TPU v7x, 32 devices: a whole 2x2x4 slice. The times are simulated.
32 devices in a mesh: track: 2 (over y), tm: 16 (over z, x, core).
Axes of the slice: x: 2, y: 2, z: 4, core: 2. Of those that a mesh axis runs over, the one named last changes fastest.
Arguments:
- track_query: bfloat16 [16, 2048, 1024], P('track', 'tm'), may hold values from -6 to 6
- track_key: bfloat16 [16, 2048, 1024], P('track', 'tm'), may hold values from -6 to 6
- track_value: bfloat16 [16, 2048, 1024], P('track', 'tm'), may hold values from -6 to 6
- log_decay: float32 [16, 8, 2048], P('track', None, 'tm'), may hold values from -2.3 to 0
- valid_length: int32 [16], replicated, may hold values from 512 to 2048, as said below
- initial_state: bfloat16 [16, 8, 128, 128], P('track'), may hold values from -24 to 24
- cross_query: bfloat16 [16, 2048, 1024], P('track', 'tm'), may hold values from -5 to 5
- cross_key: bfloat16 [16, 2048, 1024], P('track', 'tm'), may hold values from -5 to 5
- grad_out: bfloat16 [16, 2048, 1024], P('track', 'tm'), may hold values from -6 to 6
Outputs:
- grad_query: bfloat16 [16, 2048, 1024], P('track', 'tm')
- grad_key: bfloat16 [16, 2048, 1024], P('track', 'tm')
- grad_value: bfloat16 [16, 2048, 1024], P('track', 'tm')
- grad_cross_query: bfloat16 [16, 2048, 1024], P('track', 'tm')
- grad_cross_key: bfloat16 [16, 2048, 1024], P('track', 'tm')
Inputs may be any that keep to these rules, and one draw needn't show every extreme that they name: `valid_length`: multiples of 128; one track has 2048 valid steps and one has exactly 512.
All inputs are finite; a program needn't handle non-finite values.
Results may differ from a plain program's by a relative error of at most 0.005.
Values may be sent and summed in bfloat16 or wider, within the bound.
A program may use at most 256 MiB of HBM per device.

v0:
```python
import functools

import jax
import jax.numpy as jnp
from jax import lax
from jax.experimental import pallas as pl
from jax.experimental.pallas import tpu as pltpu
from jax.sharding import PartitionSpec as P

EPSILON = 1e-06
MESH = pl.DeviceIdType.MESH
BF = jnp.bfloat16
F32 = jnp.float32
TILE = 16
FAR = -1e30


def mm(a, b):
    return lax.dot_general(a, b, (((1,), (0,)), ((), ())), preferred_element_type=F32)


def mm_nt(a, b):
    return lax.dot_general(a, b, (((1,), (1,)), ((), ())), preferred_element_type=F32)


def mm_tn(a, b):
    return lax.dot_general(a, b, (((0,), (0,)), ((), ())), preferred_element_type=F32)


def remote(src, dst, send_sem, recv_sem, target):
    return pltpu.make_async_remote_copy(
        src_ref=src, dst_ref=dst, send_sem=send_sem, recv_sem=recv_sem,
        device_id=target, device_id_type=MESH,
    )


def split3(x):
    a = x.astype(BF)
    rest = x - a.astype(F32)
    b = rest.astype(BF)
    return a, b, (rest - b.astype(F32)).astype(BF)


def block_kernel(
    dims, len_ref, decay_ref, q_hbm, k_hbm, v_hbm, init_hbm, cq_hbm, ck_hbm, g_hbm,
    gq_ref, gk_ref, gv_ref, gcq_ref, gck_ref,
    q_ref, k_ref, v_ref, cq_ref, ck_ref, g_ref, init_ref,
    qo_ref, go_ref, part_send, part_recv, own_part,
    out_ref, norm_ref, state_ref, end_ref,
    sum_send, sum_recv, plane_send, plane_recv, start_send,
    e_ref, p_ref, bias_ref, gn_ref, col_ref, row_ref, ratio_ref,
    stat_own, stat_in, total_ref, dec_in, dec_plane,
    in_sem, y_send, y_recv, s_send, s_recv, r_send, r_recv,
    a_send, a_recv, b_send, b_recv, c_send, c_recv, d_send, d_recv, h_send, h_recv,
):
    groups, count, plane, heads = dims
    planes = count // plane
    tracks, rows, width = q_ref.shape
    size = width // heads
    own = tracks // plane
    tiles = rows // TILE
    span = tracks * TILE
    lanes = groups * span
    scale = 1.0 / float(size) ** 0.5
    pair = 2 if tracks % 2 == 0 else 1

    me = lax.axis_index("tm")
    mine = lax.axis_index("track")
    p = lax.rem(me, plane)
    z = me // plane
    time_first = me * rows

    def cut(h):
        return slice(h * size, (h + 1) * size)

    def plane_peer(r):
        return lax.rem(p + r, plane)

    def plane_id(peer):
        return {"tm": z * plane + peer}

    def track_id(s):
        return {"track": lax.rem(mine + s, groups)}

    hbm = (k_hbm, v_hbm, q_hbm, init_hbm.at[pl.ds(p * own, own)], ck_hbm, cq_hbm, g_hbm)
    vmem = (k_ref, v_ref, q_ref, init_ref, ck_ref, cq_ref, g_ref)
    loads = [pltpu.make_async_copy(a, b, in_sem.at[i]) for i, (a, b) in enumerate(zip(hbm, vmem))]
    for load in loads:
        load.start()

    barrier = pltpu.get_barrier_semaphore()
    for r in range(1, plane):
        pl.semaphore_signal(barrier, inc=1, device_id=plane_id(plane_peer(r)), device_id_type=MESH)
    for r in range(1, planes):
        other = lax.rem(z + r, planes) * plane + p
        pl.semaphore_signal(barrier, inc=1, device_id={"tm": other}, device_id_type=MESH)
    for s in range(1, groups):
        pl.semaphore_signal(barrier, inc=1, device_id=track_id(s), device_id_type=MESH)
    pl.semaphore_wait(barrier, plane - 1 + planes - 1 + groups - 1)

    def y_copies(h):
        return [
            remote(
                src.at[:, :, cut(h)], dst.at[s - 1, :, :, cut(h)],
                y_send.at[kind, h, s - 1], y_recv.at[kind, h, s - 1], track_id(s),
            )
            for s in range(1, groups)
            for kind, (src, dst) in enumerate(((cq_hbm, qo_ref), (g_hbm, go_ref)))
        ]

    def start_y(h):
        if h < heads:
            for copy in y_copies(h):
                copy.start()

    start_y(0)
    start_y(1)

    t_index = lax.broadcasted_iota(jnp.int32, (rows, rows), 0)
    s_index = lax.broadcasted_iota(jnp.int32, (rows, rows), 1)
    lower_mask = t_index >= s_index
    upper_mask = t_index <= s_index
    lower = jnp.where(lower_mask, 1.0, 0.0).astype(BF)
    upper = jnp.where(upper_mask, 1.0, 0.0).astype(BF)
    row_time = time_first + lax.broadcasted_iota(jnp.int32, (rows, 1), 0)

    for x in range(tracks):
        parts = split3(decay_ref[x])
        col = sum(mm_nt(lower, part) for part in parts)
        row = sum(mm(part, upper) for part in parts)
        valid = jnp.where(row_time < len_ref[mine * tracks + x], 1.0, 0.0)
        col_ref[x, :, 0:heads] = col
        col_ref[x, :, heads : 2 * heads] = jnp.exp(col)
        col_ref[x, :, 2 * heads : 3 * heads] = jnp.exp(col[rows - 1 : rows, :] - col) * valid
        col_ref[x, :, 3 * heads : 3 * heads + 1] = valid
        row_ref[x] = row
        total = jnp.broadcast_to(jnp.exp(row[:, rows - 1 : rows]), (heads, 128))
        for h in range(heads):
            at = h * own + x % own
            total_ref[x // own, at : at + 1, :] = total[h : h + 1]

    def d_copy(r):
        peer = plane_peer(r)
        return remote(
            total_ref.at[peer], dec_in.at[p], d_send.at[r - 1], d_recv.at[r - 1], plane_id(peer)
        )

    for r in range(1, plane):
        d_copy(r).start()
    dec_in[p] = total_ref[p]

    def within(x, h):
        return col_ref[x, :, h : h + 1]

    def from_start(x, h):
        return col_ref[x, :, heads + h : heads + h + 1]

    def to_end(x, h):
        return col_ref[x, :, 2 * heads + h : 2 * heads + h + 1]

    def valid_col(x):
        return col_ref[x, :, 3 * heads : 3 * heads + 1]

    def each_track(body, step=pair):
        def run(i, carry):
            for j in range(step):
                body(i * step + j)
            return carry

        lax.fori_loop(0, tracks // step, run, 0)

    def a_copy(d, h, r):
        peer = plane_peer(r)
        return remote(
            sum_send.at[h, pl.ds(peer * own, own)], sum_recv.at[d, h, p],
            a_send.at[d, h, r - 1], a_recv.at[d, h, r - 1], plane_id(peer),
        )

    def send_sums(d, h):
        for r in range(1, plane):
            a_copy(d, h, r).start()
        sum_recv[d, h, p] = sum_send[h, pl.ds(p * own, own)]

    def b_copy(d, h, r):
        target = lax.rem(z + (r if d == 0 else planes - r), planes)
        return remote(
            plane_send.at[d, h], plane_recv.at[h, z],
            b_send.at[d, h, r - 1], b_recv.at[d, h, r - 1], {"tm": target * plane + p},
        )

    def sends_plane(d, r):
        return z + r < planes if d == 0 else z - r >= 0

    def takes_plane(d, r):
        return sends_plane(1 - d, r)

    def order(d):
        return range(plane) if d == 0 else range(plane - 1, -1, -1)

    def plane_total(d, h):
        for r in range(1, plane):
            a_copy(d, h, r).wait_recv()
        for x in range(own):
            at = h * own + x
            carry = None
            for src in order(d):
                term = sum_recv[d, h, src, x].astype(F32)
                carry = term if carry is None else dec_in[src, at : at + 1, :] * carry + term
            plane_send[d, h, x] = carry.astype(BF)
        for r in range(1, planes):
            @pl.when(sends_plane(d, r))
            def _():
                b_copy(d, h, r).start()

    def c_copy(d, h, r):
        peer = plane_peer(r)
        dst = state_ref if d == 0 else end_ref
        return remote(
            start_send.at[h, peer], dst.at[h, pl.ds(p * own, own)],
            c_send.at[d, h, r - 1], c_recv.at[d, h, r - 1], plane_id(peer),
        )

    def send_states(d, h):
        for r in range(1, planes):
            @pl.when(takes_plane(d, r))
            def _():
                b_copy(d, h, r).wait_recv()
        for x in range(own):
            at = h * own + x

            def earlier(i, carry):
                src = i if d == 0 else planes - 1 - i
                return dec_plane[src, at : at + 1, :] * carry + plane_recv[h, src, x].astype(F32)

            carry = init_ref[x, h].astype(F32) if d == 0 else jnp.zeros((size, size), F32)
            carry = lax.fori_loop(0, z if d == 0 else planes - 1 - z, earlier, carry)
            for n, src in enumerate(order(d)):
                start_send[h, src, x] = carry.astype(BF)
                if n < plane - 1:
                    carry = dec_in[src, at : at + 1, :] * carry + sum_recv[d, h, src, x].astype(F32)
        for r in range(1, plane):
            c_copy(d, h, r).start()
        dst = state_ref if d == 0 else end_ref
        dst[h, pl.ds(p * own, own)] = start_send[h, p]

    def wait_states(d, h):
        for r in range(1, plane):
            c_copy(d, h, r).wait_recv()

    def drain_scan(d):
        for h in range(heads):
            for r in range(1, plane):
                a_copy(d, h, r).wait_send()
                c_copy(d, h, r).wait_send()
            for r in range(1, planes):
                @pl.when(sends_plane(d, r))
                def _():
                    b_copy(d, h, r).wait_send()

    def forward_sums(h):
        def body(x):
            key = (k_ref[x, :, cut(h)].astype(F32) * to_end(x, h)).astype(BF)
            sum_send[h, x] = mm_tn(key, v_ref[x, :, cut(h)]).astype(BF)

        each_track(body)
        send_sums(0, h)

    def forward_rows(h):
        wait_states(0, h)

        def body(x):
            q = q_ref[x, :, cut(h)]
            valid = valid_col(x)
            key = (k_ref[x, :, cut(h)].astype(F32) * valid).astype(BF)
            decay = jnp.exp(jnp.where(lower_mask, within(x, h) - row_ref[x, h : h + 1, :], FAR))
            scores = (mm_nt(q, key) * decay).astype(BF)
            outputs = mm(scores, v_ref[x, :, cut(h)]) + from_start(x, h) * mm(q, state_ref[h, x])
            square = jnp.mean(outputs * outputs, axis=-1, keepdims=True)
            inverse = lax.rsqrt(square + EPSILON) * valid
            norm_ref[x, :, cut(h)] = (outputs * inverse).astype(BF)
            out_ref[x, :, cut(h)] = outputs.astype(BF)

        each_track(body)

    def backward_sums(h):
        def body(x):
            outputs = out_ref[x, :, cut(h)].astype(F32)
            square = jnp.mean(outputs * outputs, axis=-1, keepdims=True)
            inverse = lax.rsqrt(square + EPSILON)
            unit = outputs * inverse
            grad = gn_ref[x]
            along = jnp.mean(grad * unit, axis=-1, keepdims=True)
            grad = ((inverse * valid_col(x)) * (grad - unit * along)).astype(BF)
            out_ref[x, :, cut(h)] = grad
            q_from = (q_ref[x, :, cut(h)].astype(F32) * from_start(x, h)).astype(BF)
            sum_send[h, x] = mm_tn(q_from, grad).astype(BF)

        each_track(body)
        send_sums(1, h)

    def backward_rows(h):
        wait_states(1, h)

        def body(x):
            q = q_ref[x, :, cut(h)]
            v = v_ref[x, :, cut(h)]
            valid = valid_col(x)
            key = (k_ref[x, :, cut(h)].astype(F32) * valid).astype(BF)
            grad = out_ref[x, :, cut(h)]
            end_grad = end_ref[h, x]
            decay = jnp.exp(jnp.where(upper_mask, row_ref[x, h : h + 1, :] - within(x, h), FAR))
            grad_scores = (mm_nt(v, grad) * decay).astype(BF)
            scores = (mm_nt(key, q) * decay).astype(BF)
            grad_query = mm_tn(grad_scores, key)
            grad_query = grad_query + from_start(x, h) * mm_nt(grad, state_ref[h, x])
            gq_ref[x, :, cut(h)] = grad_query.astype(BF)
            late = to_end(x, h)
            grad_key = valid * mm(grad_scores, q) + late * mm_nt(v, end_grad)
            gk_ref[x, :, cut(h)] = grad_key.astype(BF)
            grad_value = mm(scores, grad) + late * mm(key, end_grad)
            gv_ref[x, :, cut(h)] = grad_value.astype(BF)

        each_track(body)

    def shared_tables():
        row = lax.broadcasted_iota(jnp.int32, (span, 1), 0)
        lane = lax.broadcasted_iota(jnp.int32, (1, lanes), 1)
        key_length = jnp.zeros((span, 1), jnp.int32)
        for x in range(tracks):
            inside = (row >= x * TILE) & (row < (x + 1) * TILE)
            key_length = jnp.where(inside, len_ref[mine * tracks + x], key_length)
        query_length = jnp.zeros((1, lanes), jnp.int32)
        for s in range(groups):
            group = lax.rem(mine + groups - s, groups)
            for x in range(tracks):
                first = (s * tracks + x) * TILE
                inside = (lane >= first) & (lane < first + TILE)
                query_length = jnp.where(inside, len_ref[group * tracks + x], query_length)
        row_in, lane_in = lax.rem(row, TILE), lax.rem(lane, TILE)
        same = row_in == lane_in
        for tile in range(tiles):
            first = time_first + tile * TILE
            bias_ref[tile] = jnp.where(same & (first + row_in < key_length), 0.0, FAR)
            ratio_ref[2, tile : tile + 1, :] = jnp.where(first + lane_in < query_length, 1.0, 0.0)

    def gather(own_ref, other_ref, at, h):
        pieces = [own_ref[:, at, cut(h)].reshape(span, size)]
        pieces += [other_ref[s, :, at, cut(h)].reshape(span, size) for s in range(groups - 1)]
        return jnp.concatenate(pieces, axis=0)

    def each_tile(body):
        step = 2 if tiles % 2 == 0 else 1

        def run(i, carry):
            for j in range(step):
                tile = i * step + j
                body(tile, pl.ds(pl.multiple_of(tile * TILE, TILE), TILE))
            return carry

        lax.fori_loop(0, tiles // step, run, 0)

    def s_copy(h, s):
        return remote(
            stat_own.at[h], stat_in.at[s - 1, h], s_send.at[h, s - 1], s_recv.at[h, s - 1],
            track_id(s),
        )

    def cross_logits(h):
        for copy in y_copies(h):
            copy.wait_recv()
        slot = h % 2

        def body(tile, at):
            key = ck_ref[:, at, cut(h)].reshape(span, size)
            normed = norm_ref[:, at, cut(h)].reshape(span, size)
            logits = mm_nt(key, gather(cq_ref, qo_ref, at, h)) * scale + bias_ref[tile]
            top = jnp.max(logits, axis=0, keepdims=True)
            e = jnp.exp(logits - top)
            product = mm_nt(normed, gather(g_ref, go_ref, at, h))
            e_ref[slot, tile] = e
            p_ref[slot, tile] = product
            stat_own[h, 0, pl.ds(tile, 1), :] = top
            stat_own[h, 1, pl.ds(tile, 1), :] = jnp.sum(e, axis=0, keepdims=True)
            stat_own[h, 2, pl.ds(tile, 1), :] = jnp.sum(e * product, axis=0, keepdims=True)

        each_tile(body)
        for s in range(1, groups):
            s_copy(h, s).start()

    def p_copy(h, s):
        back = groups - s
        return remote(
            part_send.at[s - 1, :, :, cut(h)], part_recv.at[back - 1, :, :, cut(h)],
            r_send.at[h, s - 1], r_recv.at[h, back - 1],
            {"track": lax.rem(mine + groups - s, groups)},
        )

    def cross_grads(h):
        for s in range(1, groups):
            s_copy(h, s).wait_recv()
        slot = h % 2
        stats = [[stat_own[h, i] for i in range(3)]]
        for s in range(1, groups):
            away = (groups - s) * span
            pieces = [stat_in[s - 1, h, i] for i in range(3)]
            stats.append([jnp.concatenate([a[:, away:], a[:, :away]], axis=1) for a in pieces])
        top = functools.reduce(jnp.maximum, [a[0] for a in stats])
        weights = [jnp.exp(a[0] - top) for a in stats]
        inverse = 1.0 / sum(w * a[1] for w, a in zip(weights, stats))
        ratio_ref[0] = weights[0] * inverse * ratio_ref[2]
        ratio_ref[1] = sum(w * a[2] for w, a in zip(weights, stats)) * inverse

        def body(tile, at):
            key = ck_ref[:, at, cut(h)].reshape(span, size)
            cotangent = gather(g_ref, go_ref, at, h)
            w = e_ref[slot, tile] * ratio_ref[0, pl.ds(tile, 1), :]
            high = w.astype(BF)
            low = (w - high.astype(F32)).astype(BF)
            gn_ref[:, at, :] = (mm(high, cotangent) + mm(low, cotangent)).reshape(
                tracks, TILE, size
            )
            grad = w * ((p_ref[slot, tile] - ratio_ref[1, pl.ds(tile, 1), :]) * scale)
            grad = grad.astype(BF)
            query = gather(cq_ref, qo_ref, at, h)
            gck_ref[:, at, cut(h)] = mm(grad, query).astype(BF).reshape(tracks, TILE, size)
            parts = mm_tn(grad, key)
            own_part[:, at, cut(h)] = parts[:span].reshape(tracks, TILE, size)
            for s in range(1, groups):
                piece = parts[s * span : (s + 1) * span].astype(BF)
                part_send[s - 1, :, at, cut(h)] = piece.reshape(tracks, TILE, size)

        each_tile(body)

    def start_parts(h):
        for s in range(1, groups):
            p_copy(h, s).start()

    def add_parts(h):
        for s in range(1, groups):
            p_copy(h, s).wait_recv()

        def body(x):
            value = own_part[x, :, cut(h)]
            for s in range(groups - 1):
                value = value + part_recv[s, x, :, cut(h)].astype(F32)
            gcq_ref[x, :, cut(h)] = value.astype(BF)

        each_track(body)

    loads[0].wait()
    loads[1].wait()
    for h in range(heads):
        forward_sums(h)
    for r in range(1, plane):
        d_copy(r).wait_recv()
    whole = dec_in[0]
    for src in range(1, plane):
        whole = whole * dec_in[src]
    dec_plane[z] = whole

    def h_copy(r):
        other = lax.rem(z + r, planes) * plane + p
        return remote(
            dec_plane.at[z], dec_plane.at[z], h_send.at[r - 1], h_recv.at[r - 1], {"tm": other}
        )

    for r in range(1, planes):
        h_copy(r).start()
    start_y(2)
    shared_tables()
    loads[2].wait()
    loads[3].wait()
    for i in range(heads + 2):
        if i < heads:
            plane_total(0, i)
        if i == 0:
            for r in range(1, planes):
                h_copy(r).wait_recv()
        if 1 <= i <= heads:
            send_states(0, i - 1)
        if i >= 2:
            forward_rows(i - 2)
        if i == 4:
            start_y(3)
        if i == 7:
            start_y(4)
    for i in (4, 5, 6):
        loads[i].wait()
    drain_scan(0)

    cross_logits(0)
    for i in range(heads + 4):
        if i + 1 < heads:
            cross_logits(i + 1)
        if i < heads:
            if i == 0:
                start_y(5)
            if i == 2:
                start_y(6)
            if i == 3:
                start_y(7)
            if heads > 8 and i >= 3:
                start_y(i + 5)
            cross_grads(i)
            if i + 1 >= heads - 1:
                for h in range(heads):
                    if h == i or (i + 1 == heads - 1 and h < i):
                        start_parts(h)
            backward_sums(i)
        if 1 <= i <= heads:
            plane_total(1, i - 1)
        if 2 <= i <= heads + 1:
            send_states(1, i - 2)
        if 4 <= i:
            backward_rows(i - 4)
    for h in range(heads):
        add_parts(h)

    drain_scan(1)
    for r in range(1, plane):
        d_copy(r).wait_send()
    for r in range(1, planes):
        h_copy(r).wait_send()
    for h in range(heads):
        for copy in y_copies(h):
            copy.wait_send()
        for s in range(1, groups):
            s_copy(h, s).wait_send()
            p_copy(h, s).wait_send()


def per_device(
    count,
    groups,
    track_query,
    track_key,
    track_value,
    log_decay,
    valid_length,
    initial_state,
    cross_query,
    cross_key,
    grad_out,
):
    tracks, rows, width = track_query.shape
    heads = log_decay.shape[1]
    size = width // heads
    plane = max(n for n in (4, 2, 1) if tracks % n == 0 and count % n == 0)
    planes = count // plane
    own = tracks // plane
    tiles = rows // TILE
    span = tracks * TILE
    lanes = groups * span
    others = max(groups - 1, 1)
    peers = max(plane - 1, 1)
    layers = max(planes - 1, 1)
    vmem = pl.BlockSpec(memory_space=pltpu.VMEM)
    anywhere = pl.BlockSpec(memory_space=pl.ANY)
    wide = jax.ShapeDtypeStruct((tracks, rows, width), BF)
    block = pltpu.VMEM((tracks, rows, width), BF)
    blocks = pltpu.VMEM((others, tracks, rows, width), BF)
    states = pltpu.VMEM((heads, tracks, size, size), BF)
    dma = pltpu.SemaphoreType.DMA
    dot_flops = 2 * tracks * heads * rows * size * size
    return pl.pallas_call(
        functools.partial(block_kernel, (groups, count, plane, heads)),
        out_shape=(wide,) * 5,
        in_specs=[pl.BlockSpec(memory_space=pltpu.SMEM), vmem] + [anywhere] * 7,
        out_specs=(vmem,) * 5,
        scratch_shapes=[block] * 6
        + [pltpu.VMEM((own, heads, size, size), BF)]
        + [blocks] * 4
        + [pltpu.VMEM((tracks, rows, width), F32), block, block, states, states]
        + [
            states,
            pltpu.VMEM((2, heads, plane, own, size, size), BF),
            pltpu.VMEM((2, heads, own, size, size), BF),
            pltpu.VMEM((heads, planes, own, size, size), BF),
            pltpu.VMEM((heads, plane, own, size, size), BF),
            pltpu.VMEM((2, tiles, span, lanes), F32),
            pltpu.VMEM((2, tiles, span, lanes), F32),
            pltpu.VMEM((tiles, span, lanes), F32),
            pltpu.VMEM((tracks, rows, size), F32),
            pltpu.VMEM((tracks, rows, 128), F32),
            pltpu.VMEM((tracks, heads, rows), F32),
            pltpu.VMEM((3, tiles, lanes), F32),
            pltpu.VMEM((heads, 3, tiles, lanes), F32),
            pltpu.VMEM((others, heads, 3, tiles, lanes), F32),
            pltpu.VMEM((plane, heads * own, 128), F32),
            pltpu.VMEM((plane, heads * own, 128), F32),
            pltpu.VMEM((planes, heads * own, 128), F32),
            dma((7,)),
            dma((2, heads, others)),
            dma((2, heads, others)),
        ]
        + [dma((heads, others))] * 4
        + [dma((2, heads, peers))] * 2
        + [dma((2, heads, layers))] * 2
        + [dma((2, heads, peers))] * 2
        + [dma((peers,))] * 2
        + [dma((layers,))] * 2,
        compiler_params=pltpu.CompilerParams(
            collective_id=0, has_side_effects=True, vmem_limit_bytes=67043328
        ),
        cost_estimate=pl.CostEstimate(
            flops=20 * dot_flops, bytes_accessed=24 * tracks * rows * width, transcendentals=0
        ),
        name="block_backward",
    )(
        valid_length, log_decay, track_query, track_key, track_value, initial_state,
        cross_query, cross_key, grad_out,
    )


def solution(mesh):
    wide = P("track", "tm", None)
    return jax.shard_map(
        functools.partial(per_device, mesh.shape["tm"], mesh.shape["track"]),
        mesh=mesh,
        in_specs=(
            wide,
            wide,
            wide,
            P("track", None, "tm"),
            P(),
            P("track", None, None, None),
            wide,
            wide,
            wide,
        ),
        out_specs=(wide,) * 5,
        check_vma=False,
    )
```

profile of v0, /device:TPU:0, one launch (start us, length us, event | category | flops | bytes accessed | tf_op | source)
XLA Modules:
  0.0 188.2 jit_solution(274906271593764122)
XLA Ops:
  0.6 176.0 %block_backward.1 = (bf16[8,128,1024]{2,1,0:T(8,128)(2,1)}, bf16[8,128,1024]{2,1,0:T(8,128)(2,1)}, bf16[8,128,1024]{2,1,0:T(8,128)(2,1)}, bf16[8,128,1024]{2,1,0:T(8,128)(2,1)}, bf16[8,128,1024]{2,1,0:T(8,128)(2,1)}) custom-call(s32[16]{0:T(128)} %len_ref.1, f32[8,8,128]{2,1,0:T(8,128)} %decay_ref.1, bf16[8,128,1024]{2,1,0:T(8,128)(2,1)} %q_hbm.1, ...), custom_call_target="tpu_custom_call" | custom-call | flops 5368709120 | bytes 25165824 | tf_op jit(solution)/shard_map/block_backward/pallas_call | solution.py:565
  176.6 0.0 copy-start.3
  176.6 3.2 %copy.19 = bf16[8,128,1024]{2,1,0:T(8,128)(2,1)} copy(bf16[8,128,1024]{2,1,0:T(8,128)(2,1)} %get-tuple-element.10) | data formatting | bytes 4194304
  179.8 0.0 copy-done.3
  179.8 0.0 copy-start.2
  179.8 1.3 copy.20
  181.2 1.0 copy-done.2
  182.2 0.0 copy-start.1
  182.2 1.3 copy.21
  183.5 1.0 copy-done.1
  184.5 0.0 copy-start
  184.5 1.3 copy.22
  185.9 1.0 copy-done
  186.9 1.3 copy.23
Async XLA Ops:
  176.6 3.2 %copy-start.3 = (bf16[8,128,1024]{2,1,0:T(8,128)(2,1)S(1)}, bf16[8,128,1024]{2,1,0:T(8,128)(2,1)}, u32[]{:S(2)}) copy-start(bf16[8,128,1024]{2,1,0:T(8,128)(2,1)} %get-tuple-element.11) | copy-start | bytes 6291460
  179.8 2.3 %copy-start.2 = (bf16[8,128,1024]{2,1,0:T(8,128)(2,1)S(1)}, bf16[8,128,1024]{2,1,0:T(8,128)(2,1)}, u32[]{:S(2)}) copy-start(bf16[8,128,1024]{2,1,0:T(8,128)(2,1)} %get-tuple-element.12) | copy-start | bytes 6291460
  182.2 2.3 %copy-start.1 = (bf16[8,128,1024]{2,1,0:T(8,128)(2,1)S(1)}, bf16[8,128,1024]{2,1,0:T(8,128)(2,1)}, u32[]{:S(2)}) copy-start(bf16[8,128,1024]{2,1,0:T(8,128)(2,1)} %get-tuple-element.13) | copy-start | bytes 6291460
  184.5 2.3 %copy-start = (bf16[8,128,1024]{2,1,0:T(8,128)(2,1)S(1)}, bf16[8,128,1024]{2,1,0:T(8,128)(2,1)}, u32[]{:S(2)}) copy-start(bf16[8,128,1024]{2,1,0:T(8,128)(2,1)} %get-tuple-element.14) | copy-start | bytes 6291460
where the time goes:
time: 190 us; the launch traced here: 188 us
  Pallas kernels  176 us (93%)
  local copies, waits for them, and re-layouts  11.6 us (6%)
    pallas_call x1, Pallas kernels, per_device(): pl.pallas_call(functools.partial(block_kernel, (groups, count, plane, hea...  176 us
    unnamed x13, local copies, waits for them, and re-layouts  11.6 us

commit v1 on v0

--- a/solution.py
+++ b/solution.py
@@ -12,6 +12,7 @@
 BF = jnp.bfloat16
 F32 = jnp.float32
 TILE = 16
+VMEM_BYTES = 67043328
 FAR = -1e30
 
 
@@ -47,17 +48,18 @@
     q_ref, k_ref, v_ref, cq_ref, ck_ref, g_ref, init_ref,
     qo_ref, go_ref, part_send, part_recv, own_part,
     out_ref, norm_ref, state_ref, end_ref,
-    sum_send, sum_recv, plane_send, plane_recv, start_send,
+    sum_send, core_recv, chip_send, chip_own, chip_recv, relay_send, relay_recv,
+    x_start, chip_start, core_start,
     e_ref, p_ref, bias_ref, gn_ref, col_ref, row_ref, ratio_ref,
-    stat_own, stat_in, total_ref, dec_in, dec_plane,
-    in_sem, y_send, y_recv, s_send, s_recv, r_send, r_recv,
-    a_send, a_recv, b_send, b_recv, c_send, c_recv, d_send, d_recv, h_send, h_recv,
+    stat_own, stat_in, total_ref, core_total, chip_total, factor_ref,
+    in_sem, y_send, y_recv, s_send, s_recv, r_send, r_recv, scan_send, scan_recv, d_send, d_recv,
 ):
-    groups, count, plane, heads = dims
-    planes = count // plane
+    groups, count, cores, chips, heads = dims
+    planes = count // (cores * chips)
     tracks, rows, width = q_ref.shape
     size = width // heads
-    own = tracks // plane
+    half = tracks // cores
+    own = half // chips
     tiles = rows // TILE
     span = tracks * TILE
     lanes = groups * span
@@ -66,37 +68,50 @@
 
     me = lax.axis_index("tm")
     mine = lax.axis_index("track")
-    p = lax.rem(me, plane)
-    z = me // plane
+    c = lax.rem(me, cores)
+    chip = lax.rem(me // cores, chips)
+    z = me // (cores * chips)
+    mine_first = c * half + chip * own
     time_first = me * rows
 
     def cut(h):
         return slice(h * size, (h + 1) * size)
 
-    def plane_peer(r):
-        return lax.rem(p + r, plane)
-
-    def plane_id(peer):
-        return {"tm": z * plane + peer}
+    def place(plane, column, core):
+        return {"tm": (plane * chips + column) * cores + core}
+
+    core_id = place(z, chip, lax.rem(c + 1, cores))
+    chip_id = place(z, lax.rem(chip + 1, chips), c)
+
+    def relay_id(d):
+        return place(lax.rem(z + (1 if d == 0 else planes - 1), planes), chip, c)
+
+    def first_plane(d):
+        return z == (0 if d == 0 else planes - 1)
 
     def track_id(s):
         return {"track": lax.rem(mine + s, groups)}
 
-    hbm = (k_hbm, v_hbm, q_hbm, init_hbm.at[pl.ds(p * own, own)], ck_hbm, cq_hbm, g_hbm)
+    hbm = (k_hbm, v_hbm, q_hbm, init_hbm.at[pl.ds(mine_first, own)], ck_hbm, cq_hbm, g_hbm)
     vmem = (k_ref, v_ref, q_ref, init_ref, ck_ref, cq_ref, g_ref)
     loads = [pltpu.make_async_copy(a, b, in_sem.at[i]) for i, (a, b) in enumerate(zip(hbm, vmem))]
     for load in loads:
         load.start()
 
     barrier = pltpu.get_barrier_semaphore()
-    for r in range(1, plane):
-        pl.semaphore_signal(barrier, inc=1, device_id=plane_id(plane_peer(r)), device_id_type=MESH)
-    for r in range(1, planes):
-        other = lax.rem(z + r, planes) * plane + p
-        pl.semaphore_signal(barrier, inc=1, device_id={"tm": other}, device_id_type=MESH)
-    for s in range(1, groups):
-        pl.semaphore_signal(barrier, inc=1, device_id=track_id(s), device_id_type=MESH)
-    pl.semaphore_wait(barrier, plane - 1 + planes - 1 + groups - 1)
+    peers = [track_id(s) for s in range(1, groups)]
+    if cores > 1:
+        peers.append(core_id)
+    if chips > 1:
+        peers.append(chip_id)
+    for peer in peers:
+        pl.semaphore_signal(barrier, inc=1, device_id=peer, device_id_type=MESH)
+    for d in range(2):
+        @pl.when(jnp.logical_not(first_plane(1 - d)))
+        def _():
+            pl.semaphore_signal(barrier, inc=1, device_id=relay_id(d), device_id_type=MESH)
+    inner = jnp.where(first_plane(0), 0, 1) + jnp.where(first_plane(1), 0, 1)
+    pl.semaphore_wait(barrier, len(peers) + inner)
 
     def y_copies(h):
         return [
@@ -113,8 +128,8 @@
             for copy in y_copies(h):
                 copy.start()
 
-    start_y(0)
-    start_y(1)
+    for h in range(4):
+        start_y(h)
 
     t_index = lax.broadcasted_iota(jnp.int32, (rows, rows), 0)
     s_index = lax.broadcasted_iota(jnp.int32, (rows, rows), 1)
@@ -136,18 +151,17 @@
         row_ref[x] = row
         total = jnp.broadcast_to(jnp.exp(row[:, rows - 1 : rows]), (heads, 128))
         for h in range(heads):
-            at = h * own + x % own
-            total_ref[x // own, at : at + 1, :] = total[h : h + 1]
-
-    def d_copy(r):
-        peer = plane_peer(r)
-        return remote(
-            total_ref.at[peer], dec_in.at[p], d_send.at[r - 1], d_recv.at[r - 1], plane_id(peer)
-        )
-
-    for r in range(1, plane):
-        d_copy(r).start()
-    dec_in[p] = total_ref[p]
+            at = h * half + x % half
+            total_ref[x // half, at : at + 1, :] = total[h : h + 1]
+
+    def d_copy(level):
+        if level == 0:
+            other = lax.rem(c + 1, cores)
+            return remote(total_ref.at[other], core_total, d_send.at[0], d_recv.at[0], core_id)
+        return remote(chip_total.at[0], chip_total.at[1], d_send.at[1], d_recv.at[1], chip_id)
+
+    if cores > 1:
+        d_copy(0).start()
 
     def within(x, h):
         return col_ref[x, :, h : h + 1]
@@ -169,93 +183,150 @@
 
         lax.fori_loop(0, tracks // step, run, 0)
 
-    def a_copy(d, h, r):
-        peer = plane_peer(r)
-        return remote(
-            sum_send.at[h, pl.ds(peer * own, own)], sum_recv.at[d, h, p],
-            a_send.at[d, h, r - 1], a_recv.at[d, h, r - 1], plane_id(peer),
-        )
+    def level_factors(level, earlier, own_decay, other_decay):
+        for d in range(2):
+            first = earlier(d)
+            one, none = jnp.ones_like(own_decay), jnp.zeros_like(own_decay)
+            factor_ref[level, d, 0] = jnp.where(first, other_decay, one)
+            factor_ref[level, d, 1] = jnp.where(first, one, own_decay)
+            factor_ref[level, d, 2] = jnp.where(first, one, other_decay)
+            factor_ref[level, d, 3] = jnp.where(first, none, one)
+            factor_ref[level, d, 4] = jnp.where(first, own_decay, one)
+            factor_ref[level, d, 5] = jnp.where(first, one, none)
+
+    def core_factors():
+        own_decay = total_ref[c]
+        whole = own_decay
+        if cores > 1:
+            d_copy(0).wait_recv()
+            other_decay = core_total[...]
+            whole = own_decay * other_decay
+            level_factors(0, lambda d: c == (0 if d == 0 else 1), own_decay, other_decay)
+        chip_total[0] = whole
+        if chips > 1:
+            d_copy(1).start()
+
+    def chip_factors():
+        whole = chip_total[0]
+        if chips > 1:
+            d_copy(1).wait_recv()
+            level_factors(1, lambda d: chip == (0 if d == 0 else 1), whole, chip_total[1])
+            whole = whole * chip_total[1]
+        chip_total[2] = whole
+
+    def factors(level, d, at):
+        return [factor_ref[level, d, i, at, :] for i in range(6)]
+
+    def scan_copy(kind, d, h):
+        dst_state = state_ref if d == 0 else end_ref
+        src, dst, target = {
+            0: lambda: (
+                sum_send.at[h, pl.ds(lax.rem(c + 1, cores) * half, half)], core_recv.at[d, h], core_id
+            ),
+            1: lambda: (chip_send.at[h], chip_recv.at[d, h], chip_id),
+            2: lambda: (relay_send.at[h], relay_recv.at[d, h], relay_id(d)),
+            3: lambda: (x_start.at[h], chip_start.at[d, h, pl.ds(chip * own, own)], chip_id),
+            4: lambda: (core_start.at[h], dst_state.at[h, pl.ds(c * half, half)], core_id),
+        }[kind]()
+        return remote(src, dst, scan_send.at[kind, d, h], scan_recv.at[kind, d, h], target)
 
     def send_sums(d, h):
-        for r in range(1, plane):
-            a_copy(d, h, r).start()
-        sum_recv[d, h, p] = sum_send[h, pl.ds(p * own, own)]
-
-    def b_copy(d, h, r):
-        target = lax.rem(z + (r if d == 0 else planes - r), planes)
-        return remote(
-            plane_send.at[d, h], plane_recv.at[h, z],
-            b_send.at[d, h, r - 1], b_recv.at[d, h, r - 1], {"tm": target * plane + p},
-        )
-
-    def sends_plane(d, r):
-        return z + r < planes if d == 0 else z - r >= 0
-
-    def takes_plane(d, r):
-        return sends_plane(1 - d, r)
-
-    def order(d):
-        return range(plane) if d == 0 else range(plane - 1, -1, -1)
-
-    def plane_total(d, h):
-        for r in range(1, plane):
-            a_copy(d, h, r).wait_recv()
-        for x in range(own):
-            at = h * own + x
-            carry = None
-            for src in order(d):
-                term = sum_recv[d, h, src, x].astype(F32)
-                carry = term if carry is None else dec_in[src, at : at + 1, :] * carry + term
-            plane_send[d, h, x] = carry.astype(BF)
-        for r in range(1, planes):
-            @pl.when(sends_plane(d, r))
+        if cores > 1:
+            scan_copy(0, d, h).start()
+
+    def chip_sums(d, h):
+        if cores > 1:
+            scan_copy(0, d, h).wait_recv()
+
+        def sum_of(j):
+            mine_sum = sum_send[h, c * half + j].astype(F32)
+            if cores == 1:
+                return mine_sum
+            f = factors(0, d, pl.ds(h * half + j, 1))
+            return f[0] * mine_sum + f[1] * core_recv[d, h, j].astype(F32)
+
+        if chips > 1:
+            other = lax.rem(chip + 1, chips)
+            for i in range(own):
+                chip_send[h, i] = sum_of(other * own + i).astype(BF)
+            scan_copy(1, d, h).start()
+        for i in range(own):
+            chip_own[h, i] = sum_of(chip * own + i)
+
+    def relay(d, h):
+        if chips > 1:
+            scan_copy(1, d, h).wait_recv()
+
+        @pl.when(first_plane(d))
+        def _():
+            for i in range(own):
+                start = init_ref[i, h].astype(F32) if d == 0 else jnp.zeros((size, size), F32)
+                relay_recv[d, h, i] = start
+
+        if planes > 1:
+            @pl.when(jnp.logical_not(first_plane(d)))
             def _():
-                b_copy(d, h, r).start()
-
-    def c_copy(d, h, r):
-        peer = plane_peer(r)
+                scan_copy(2, d, h).wait_recv()
+
+        for i in range(own):
+            at = pl.ds(h * half + chip * own + i, 1)
+            start = relay_recv[d, h, i]
+            total = chip_own[h, i]
+            here = start
+            if chips > 1:
+                f = factors(1, d, at)
+                away = chip_recv[d, h, i].astype(F32)
+                x_start[h, i] = (f[4] * start + f[5] * total).astype(BF)
+                here = f[2] * start + f[3] * away
+                total = f[0] * total + f[1] * away
+            relay_send[h, i] = chip_total[2, at, :] * start + total
+            chip_start[d, h, chip * own + i] = here.astype(BF)
+        if planes > 1:
+            @pl.when(jnp.logical_not(first_plane(1 - d)))
+            def _():
+                scan_copy(2, d, h).start()
+        if chips > 1:
+            scan_copy(3, d, h).start()
+
+    def core_states(d, h):
+        if chips > 1:
+            x_copy = remote(
+                x_start.at[h], chip_start.at[d, h, pl.ds(lax.rem(chip + 1, chips) * own, own)],
+                scan_send.at[3, d, h], scan_recv.at[3, d, h], chip_id,
+            )
+            x_copy.wait_recv()
         dst = state_ref if d == 0 else end_ref
-        return remote(
-            start_send.at[h, peer], dst.at[h, pl.ds(p * own, own)],
-            c_send.at[d, h, r - 1], c_recv.at[d, h, r - 1], plane_id(peer),
-        )
-
-    def send_states(d, h):
-        for r in range(1, planes):
-            @pl.when(takes_plane(d, r))
-            def _():
-                b_copy(d, h, r).wait_recv()
-        for x in range(own):
-            at = h * own + x
-
-            def earlier(i, carry):
-                src = i if d == 0 else planes - 1 - i
-                return dec_plane[src, at : at + 1, :] * carry + plane_recv[h, src, x].astype(F32)
-
-            carry = init_ref[x, h].astype(F32) if d == 0 else jnp.zeros((size, size), F32)
-            carry = lax.fori_loop(0, z if d == 0 else planes - 1 - z, earlier, carry)
-            for n, src in enumerate(order(d)):
-                start_send[h, src, x] = carry.astype(BF)
-                if n < plane - 1:
-                    carry = dec_in[src, at : at + 1, :] * carry + sum_recv[d, h, src, x].astype(F32)
-        for r in range(1, plane):
-            c_copy(d, h, r).start()
-        dst = state_ref if d == 0 else end_ref
-        dst[h, pl.ds(p * own, own)] = start_send[h, p]
+        for j in range(half):
+            start = chip_start[d, h, j].astype(F32)
+            if cores == 1:
+                dst[h, j] = start.astype(BF)
+                continue
+            f = factors(0, d, pl.ds(h * half + j, 1))
+            mine_sum = sum_send[h, c * half + j].astype(F32)
+            core_start[h, j] = (f[4] * start + f[5] * mine_sum).astype(BF)
+            dst[h, c * half + j] = (f[2] * start + f[3] * core_recv[d, h, j].astype(F32)).astype(BF)
+        if cores > 1:
+            scan_copy(4, d, h).start()
 
     def wait_states(d, h):
-        for r in range(1, plane):
-            c_copy(d, h, r).wait_recv()
+        if cores > 1:
+            other = lax.rem(c + 1, cores)
+            dst = state_ref if d == 0 else end_ref
+            remote(
+                core_start.at[h], dst.at[h, pl.ds(other * half, half)],
+                scan_send.at[4, d, h], scan_recv.at[4, d, h], core_id,
+            ).wait_recv()
 
     def drain_scan(d):
         for h in range(heads):
-            for r in range(1, plane):
-                a_copy(d, h, r).wait_send()
-                c_copy(d, h, r).wait_send()
-            for r in range(1, planes):
-                @pl.when(sends_plane(d, r))
-                def _():
-                    b_copy(d, h, r).wait_send()
+            for kind in range(5):
+                if kind == 2:
+                    if planes > 1:
+                        @pl.when(jnp.logical_not(first_plane(1 - d)))
+                        def _():
+                            scan_copy(kind, d, h).wait_send()
+                elif (cores if kind in (0, 4) else chips) > 1:
+                    scan_copy(kind, d, h).wait_send()
 
     def forward_sums(h):
         def body(x):
@@ -449,84 +520,84 @@
 
     loads[0].wait()
     loads[1].wait()
+    core_factors()
     for h in range(heads):
         forward_sums(h)
-    for r in range(1, plane):
-        d_copy(r).wait_recv()
-    whole = dec_in[0]
-    for src in range(1, plane):
-        whole = whole * dec_in[src]
-    dec_plane[z] = whole
-
-    def h_copy(r):
-        other = lax.rem(z + r, planes) * plane + p
-        return remote(
-            dec_plane.at[z], dec_plane.at[z], h_send.at[r - 1], h_recv.at[r - 1], {"tm": other}
-        )
-
-    for r in range(1, planes):
-        h_copy(r).start()
-    start_y(2)
-    shared_tables()
+        if h == 0:
+            chip_factors()
+        if h >= 1:
+            chip_sums(0, h - 1)
+    chip_sums(0, heads - 1)
     loads[2].wait()
     loads[3].wait()
-    for i in range(heads + 2):
+    relay(0, 0)
+    relay(0, 1)
+    shared_tables()
+    for i in range(heads + 1):
+        if i + 2 < heads:
+            relay(0, i + 2)
         if i < heads:
-            plane_total(0, i)
-        if i == 0:
-            for r in range(1, planes):
-                h_copy(r).wait_recv()
-        if 1 <= i <= heads:
-            send_states(0, i - 1)
-        if i >= 2:
-            forward_rows(i - 2)
-        if i == 4:
-            start_y(3)
-        if i == 7:
+            core_states(0, i)
+        if i >= 1:
+            forward_rows(i - 1)
+        if i == 2:
             start_y(4)
+        if i == 6:
+            start_y(5)
     for i in (4, 5, 6):
         loads[i].wait()
     drain_scan(0)
 
     cross_logits(0)
-    for i in range(heads + 4):
+    for i in range(heads + 2):
+        if 1 <= i <= heads:
+            chip_sums(1, i - 1)
         if i + 1 < heads:
             cross_logits(i + 1)
         if i < heads:
-            if i == 0:
-                start_y(5)
+            if i == 1:
+                start_y(6)
             if i == 2:
-                start_y(6)
-            if i == 3:
                 start_y(7)
-            if heads > 8 and i >= 3:
-                start_y(i + 5)
+            if heads > 8 and i >= 2:
+                start_y(i + 6)
             cross_grads(i)
-            if i + 1 >= heads - 1:
-                for h in range(heads):
-                    if h == i or (i + 1 == heads - 1 and h < i):
-                        start_parts(h)
             backward_sums(i)
+            if i == heads - 3:
+                start_parts(0)
+            if i >= heads - 2:
+                for h in range(1 if i == heads - 2 else i, i + 1):
+                    start_parts(h)
+        if i >= 3:
+            backward_rows(i - 3)
         if 1 <= i <= heads:
-            plane_total(1, i - 1)
-        if 2 <= i <= heads + 1:
-            send_states(1, i - 2)
-        if 4 <= i:
-            backward_rows(i - 4)
+            relay(1, i - 1)
+        if i >= 2:
+            core_states(1, i - 2)
+    for h in range(heads - 1, heads):
+        backward_rows(h)
     for h in range(heads):
         add_parts(h)
 
     drain_scan(1)
-    for r in range(1, plane):
-        d_copy(r).wait_send()
-    for r in range(1, planes):
-        h_copy(r).wait_send()
+    if cores > 1:
+        d_copy(0).wait_send()
+    if chips > 1:
+        d_copy(1).wait_send()
     for h in range(heads):
         for copy in y_copies(h):
             copy.wait_send()
         for s in range(1, groups):
             s_copy(h, s).wait_send()
             p_copy(h, s).wait_send()
+
+
+def write_kernel(*refs):
+    copies = [pltpu.make_async_copy(refs[i], refs[5 + i], refs[10].at[i]) for i in range(5)]
+    for copy in copies:
+        copy.start()
+    for copy in copies:
+        copy.wait()
 
 
 def per_device(
@@ -545,15 +616,14 @@
     tracks, rows, width = track_query.shape
     heads = log_decay.shape[1]
     size = width // heads
-    plane = max(n for n in (4, 2, 1) if tracks % n == 0 and count % n == 0)
-    planes = count // plane
-    own = tracks // plane
+    cores = 2 if tracks % 2 == 0 and count % 2 == 0 else 1
+    half = tracks // cores
+    chips = 2 if half % 2 == 0 and count % (2 * cores) == 0 else 1
+    own = half // chips
     tiles = rows // TILE
     span = tracks * TILE
     lanes = groups * span
     others = max(groups - 1, 1)
-    peers = max(plane - 1, 1)
-    layers = max(planes - 1, 1)
     vmem = pl.BlockSpec(memory_space=pltpu.VMEM)
     anywhere = pl.BlockSpec(memory_space=pl.ANY)
     wide = jax.ShapeDtypeStruct((tracks, rows, width), BF)
@@ -562,9 +632,9 @@
     states = pltpu.VMEM((heads, tracks, size, size), BF)
     dma = pltpu.SemaphoreType.DMA
     dot_flops = 2 * tracks * heads * rows * size * size
-    return pl.pallas_call(
-        functools.partial(block_kernel, (groups, count, plane, heads)),
-        out_shape=(wide,) * 5,
+    results = pl.pallas_call(
+        functools.partial(block_kernel, (groups, count, cores, chips, heads)),
+        out_shape=(pltpu.VMEM(wide.shape, BF),) * 5,
         in_specs=[pl.BlockSpec(memory_space=pltpu.SMEM), vmem] + [anywhere] * 7,
         out_specs=(vmem,) * 5,
         scratch_shapes=[block] * 6
@@ -573,10 +643,15 @@
         + [pltpu.VMEM((tracks, rows, width), F32), block, block, states, states]
         + [
             states,
-            pltpu.VMEM((2, heads, plane, own, size, size), BF),
+            pltpu.VMEM((2, heads, half, size, size), BF),
+            pltpu.VMEM((heads, own, size, size), BF),
+            pltpu.VMEM((heads, own, size, size), F32),
             pltpu.VMEM((2, heads, own, size, size), BF),
-            pltpu.VMEM((heads, planes, own, size, size), BF),
-            pltpu.VMEM((heads, plane, own, size, size), BF),
+            pltpu.VMEM((heads, own, size, size), F32),
+            pltpu.VMEM((2, heads, own, size, size), F32),
+            pltpu.VMEM((heads, own, size, size), BF),
+            pltpu.VMEM((2, heads, half, size, size), BF),
+            pltpu.VMEM((heads, half, size, size), BF),
             pltpu.VMEM((2, tiles, span, lanes), F32),
             pltpu.VMEM((2, tiles, span, lanes), F32),
             pltpu.VMEM((tiles, span, lanes), F32),
@@ -586,21 +661,19 @@
             pltpu.VMEM((3, tiles, lanes), F32),
             pltpu.VMEM((heads, 3, tiles, lanes), F32),
             pltpu.VMEM((others, heads, 3, tiles, lanes), F32),
-            pltpu.VMEM((plane, heads * own, 128), F32),
-            pltpu.VMEM((plane, heads * own, 128), F32),
-            pltpu.VMEM((planes, heads * own, 128), F32),
+            pltpu.VMEM((cores, heads * half, 128), F32),
+            pltpu.VMEM((heads * half, 128), F32),
+            pltpu.VMEM((3, heads * half, 128), F32),
+            pltpu.VMEM((2, 2, 6, heads * half, 128), F32),
             dma((7,)),
             dma((2, heads, others)),
             dma((2, heads, others)),
         ]
         + [dma((heads, others))] * 4
-        + [dma((2, heads, peers))] * 2
-        + [dma((2, heads, layers))] * 2
-        + [dma((2, heads, peers))] * 2
-        + [dma((peers,))] * 2
-        + [dma((layers,))] * 2,
+        + [dma((5, 2, heads))] * 2
+        + [dma((2,))] * 2,
         compiler_params=pltpu.CompilerParams(
-            collective_id=0, has_side_effects=True, vmem_limit_bytes=67043328
+            collective_id=0, has_side_effects=True, vmem_limit_bytes=VMEM_BYTES - 5 * wide.size * 2
         ),
         cost_estimate=pl.CostEstimate(
             flops=20 * dot_flops, bytes_accessed=24 * tracks * rows * width, transcendentals=0
@@ -610,6 +683,15 @@
         valid_length, log_decay, track_query, track_key, track_value, initial_state,
         cross_query, cross_key, grad_out,
     )
+    return pl.pallas_call(
+        write_kernel,
+        out_shape=(wide,) * 5,
+        in_specs=[vmem] * 5,
+        out_specs=(anywhere,) * 5,
+        scratch_shapes=[dma((5,))],
+        compiler_params=pltpu.CompilerParams(vmem_limit_bytes=2**20),
+        name="write_results",
+    )(*results)
 
 
 def solution(mesh):

time: 190 us -> 185 us (0.974); the launches traced: 188 us -> 185 us
  local copies, waits for them, and re-layouts: 11.6 us -> 0 us
  Pallas kernels: 176 us -> 184 us
    unnamed x13 -> x0, local copies, waits for them, and re-layouts: 11.6 us -> none
    pallas_call x1 -> x2, Pallas kernels: 176 us -> 184 us  [the longest x1 180 us: per_device(): pl.pallas_call(functools.partial(block_kernel, (groups, count, cores, chi...]
where the time goes in v1:
time: 185 us
  Pallas kernels  184 us (99%)
    pallas_call x1, Pallas kernels, per_device(): pl.pallas_call(functools.partial(block_kernel, (groups, count, cores, chi...  180 us
    pallas_call x1, Pallas kernels, per_device(): pl.pallas_call(write_kernel, out_shape=(wide,) * 5, in_specs=[vmem] * 5,...  4.01 us

profile of v1, /device:TPU:0, one launch (start us, length us, event | category | flops | bytes accessed | tf_op | source)
XLA Modules:
  0.0 185.2 jit_solution(6073512013959922039)
XLA Ops:
  0.6 180.4 %block_backward.1 = (bf16[8,128,1024]{2,1,0:T(8,128)(2,1)S(1)}, bf16[8,128,1024]{2,1,0:T(8,128)(2,1)S(1)}, bf16[8,128,1024]{2,1,0:T(8,128)(2,1)S(1)}, bf16[8,128...) custom-call(s32[16]{0:T(128)} %len_ref.1, f32[8,8,128]{2,1,0:T(8,128)} %decay_ref.1, bf16[8,128,1024]{2,1,0:T(8,128)(2,1)} %q_hbm.1, ...), custom_call_target="tpu_custom_call" | custom-call | flops 5368709120 | bytes 25165824 | tf_op jit(solution)/shard_map/block_backward/pallas_call | solution.py:635
  181.0 4.0 %write_results.1 = (bf16[8,128,1024]{2,1,0:T(8,128)(2,1)}, bf16[8,128,1024]{2,1,0:T(8,128)(2,1)}, bf16[8,128,1024]{2,1,0:T(8,128)(2,1)}, bf16[8,128,1024]{2,1,0:T(8,128)(2,1)}, bf16[8,128,1024]{2,1,0:T(8,128)(2,1)}) custom-call(bf16[8,128,1024]{2,1,0:T(8,128)(2,1)S(1)} %get-tuple-element.10.refs_0_, bf16[8,128,1024]{2,1,0:T(8,128)(2,1)S(1)} %get-tuple-element.11.refs_1_, ...), custom_call_target="tpu_custom_call" | custom-call | tf_op jit(solution)/shard_map/write_results/pallas_call | solution.py:686

commit v2 on v1

--- a/solution.py
+++ b/solution.py
@@ -549,33 +549,37 @@
     drain_scan(0)
 
     cross_logits(0)
-    for i in range(heads + 2):
+    lag = planes - 1
+    sent = 0
+    for i in range(heads + lag + 3):
         if 1 <= i <= heads:
             chip_sums(1, i - 1)
         if i + 1 < heads:
             cross_logits(i + 1)
         if i < heads:
-            if i == 1:
+            if i == 0:
                 start_y(6)
             if i == 2:
                 start_y(7)
             if heads > 8 and i >= 2:
                 start_y(i + 6)
             cross_grads(i)
+            ready = {3: 1, 2: 2, 1: 4, 0: heads - 1}.get(heads - 2 - i, 0) if i < heads - 1 else heads
+            ready = min(ready, i + 1)
+            while sent < ready:
+                start_parts(sent)
+                sent += 1
             backward_sums(i)
-            if i == heads - 3:
-                start_parts(0)
-            if i >= heads - 2:
-                for h in range(1 if i == heads - 2 else i, i + 1):
-                    start_parts(h)
-        if i >= 3:
-            backward_rows(i - 3)
-        if 1 <= i <= heads:
-            relay(1, i - 1)
-        if i >= 2:
-            core_states(1, i - 2)
-    for h in range(heads - 1, heads):
-        backward_rows(h)
+        if 0 <= i - lag - 3:
+            backward_rows(i - lag - 3)
+        if 1 <= i <= heads + lag:
+            h = i - 1 - (lag - z)
+
+            @pl.when((h >= 0) & (h < heads))
+            def _():
+                relay(1, h)
+        if 0 <= i - lag - 2 < heads:
+            core_states(1, i - lag - 2)
     for h in range(heads):
         add_parts(h)
 

time: 185 us -> 164 us (0.89)
  Pallas kernels: 184 us -> 162 us
    pallas_call x1, Pallas kernels: 180 us -> 158 us  [per_device(): pl.pallas_call(functools.partial(block_kernel, (groups, count, cores, chi...]
where the time goes in v2:
time: 164 us; the launch traced here: 163 us
  Pallas kernels  162 us (99%)
    pallas_call x1, Pallas kernels, per_device(): pl.pallas_call(functools.partial(block_kernel, (groups, count, cores, chi...  158 us
    pallas_call x1, Pallas kernels, per_device(): pl.pallas_call(write_kernel, out_shape=(wide,) * 5, in_specs=[vmem] * 5,...  4.01 us

profile of v2, /device:TPU:0, one launch (start us, length us, event | category | flops | bytes accessed | tf_op | source)
XLA Modules:
  0.0 163.1 jit_solution(17880394856339064961)
XLA Ops:
  0.6 158.3 %block_backward.1 = (bf16[8,128,1024]{2,1,0:T(8,128)(2,1)S(1)}, bf16[8,128,1024]{2,1,0:T(8,128)(2,1)S(1)}, bf16[8,128,1024]{2,1,0:T(8,128)(2,1)S(1)}, bf16[8,128...) custom-call(s32[16]{0:T(128)} %len_ref.1, f32[8,8,128]{2,1,0:T(8,128)} %decay_ref.1, bf16[8,128,1024]{2,1,0:T(8,128)(2,1)} %q_hbm.1, ...), custom_call_target="tpu_custom_call" | custom-call | flops 5368709120 | bytes 25165824 | tf_op jit(solution)/shard_map/block_backward/pallas_call | solution.py:639
  158.9 4.0 %write_results.1 = (bf16[8,128,1024]{2,1,0:T(8,128)(2,1)}, bf16[8,128,1024]{2,1,0:T(8,128)(2,1)}, bf16[8,128,1024]{2,1,0:T(8,128)(2,1)}, bf16[8,128,1024]{2,1,0:T(8,128)(2,1)}, bf16[8,128,1024]{2,1,0:T(8,128)(2,1)}) custom-call(bf16[8,128,1024]{2,1,0:T(8,128)(2,1)S(1)} %get-tuple-element.10.refs_0_, bf16[8,128,1024]{2,1,0:T(8,128)(2,1)S(1)} %get-tuple-element.11.refs_1_, ...), custom_call_target="tpu_custom_call" | custom-call | tf_op jit(solution)/shard_map/write_results/pallas_call | solution.py:690
